TPU v7x, 256 devices: a whole 4x4x8 slice. The times are simulated.
256 devices in a mesh: row: 64 (over y, z, core), col: 4 (over x).
Axes of the slice: x: 4, y: 4, z: 8, core: 2. Of those that a mesh axis runs over, the one named last changes fastest.
Arguments:
- features: bfloat16 [65536, 256], P('row', 'col'), may hold values from -600 to 600
- tile_vals: bfloat16 [10240, 128, 128], P('row'), may hold values from -0.125 to 0.125
- tile_rows: int32 [64, 160], P('row'), may hold values from 0 to 7
- tile_srcs: int32 [64, 160], P('row'), may hold values from 0 to 135, as said below
- tile_count: int32 [64], P('row'), may hold values from 20 to 160, as said below
- needed: int32 [64, 64, 2], P('row'), may hold values from 0 to 7, as said below
- hop_noise: float32 [2, 65536, 256], P(None, 'row', 'col'), may hold values from -0.24 to 0.24
- enc_weight: bfloat16 [3, 256, 256], replicated, may hold values from -3.59375 to 3.59375
Outputs:
- encoded: bfloat16 [65536, 256], P('row', 'col')
Inputs may be any that keep to these rules, and one draw needn't show every extreme that they name: `tile_count`: some row index has exactly 160 live slots; slots at or beyond a row index's count are ignored. `tile_srcs`: A value s below 8 names the row index's own block s; otherwise s = 8 + o * 2 + c names entry c of needed for owner o, and o is never the row index itself. needed[d, o, :] are 2 distinct block indices among owner o's 8 blocks.
All inputs are finite; a program needn't handle non-finite values.
Results may differ from a plain program's by a relative error of at most 0.0053.
Values may be sent and summed in bfloat16 or wider, within the bound.
No kernel may reach another device: no remote copies, remote signals or barrier semaphores. Data moves between devices by JAX's collectives and lax.ppermute only.
A program may use at most 64 MiB of HBM per device.

v0:
```python
import jax
import jax.numpy as jnp
from jax import lax
from jax.sharding import PartitionSpec as P

BLK = 128
BPD = 8
TPD = 160
CAP = 2
HOPS = 2
epsilon = 1e-06


def shards(features, tile_vals, tile_rows, tile_srcs, tile_count, needed, hop_noise, enc_weight):
    row_count = lax.axis_size("row")
    row_index = lax.axis_index("row")
    col_index = lax.axis_index("col")
    local_rows, local_width = features.shape
    sources = tile_srcs[0]
    block_rows = tile_rows[0]
    live_count = tile_count[0]
    wanted = needed[0]
    tile_order = jnp.arange(TPD, dtype=jnp.int32)
    onehot = (
        (block_rows[:, None] == jnp.arange(BPD, dtype=jnp.int32)[None, :])
        & (tile_order < live_count)[:, None]
    ).astype(jnp.float32)

    def normalize(values):
        squares = lax.psum(jnp.sum(values * values, axis=1), "col")
        return (values / jnp.sqrt(squares + epsilon)[:, None]).astype(jnp.bfloat16)

    remote = jnp.maximum(sources - BPD, 0)
    slot_table = wanted.reshape(-1)
    looked_up = jnp.sum(
        jnp.where(
            remote[:, None] == jnp.arange(row_count * CAP, dtype=jnp.int32)[None, :],
            slot_table[None, :],
            0,
        ),
        axis=1,
    )
    global_block = jnp.where(
        sources < BPD, row_index * BPD + sources, remote // CAP * BPD + looked_up
    )
    current = normalize(features.astype(jnp.float32))
    layers = [current]
    for hop_index in range(HOPS):
        whole = lax.all_gather(current.reshape(BPD, BLK * local_width), "row", axis=0, tiled=True)
        products = jnp.einsum(
            "tij,tjf->tif",
            tile_vals,
            jnp.take(whole, global_block, axis=0).reshape(TPD, BLK, local_width),
            preferred_element_type=jnp.float32,
        )
        summed = jnp.einsum("tr,tif->rif", onehot, products, precision=lax.Precision.HIGHEST)
        current = normalize(summed.reshape(local_rows, local_width) + hop_noise[hop_index])
        layers.append(current)
    stacked = jnp.stack(layers)
    weight_slice = lax.dynamic_slice_in_dim(
        enc_weight, col_index * local_width, local_width, axis=1
    )
    terms = jnp.einsum("kri,kio->ro", stacked, weight_slice, preferred_element_type=jnp.float32)
    encoded = lax.psum_scatter(terms, "col", scatter_dimension=1, tiled=True)
    return encoded.astype(jnp.bfloat16)


def solution(mesh):
    in_specs = (
        P("row", "col"),
        P("row", None, None),
        P("row", None),
        P("row", None),
        P("row"),
        P("row", None, None),
        P(None, "row", "col"),
        P(),
    )
    out_specs = P("row", "col")
    return jax.shard_map(shards, mesh=mesh, in_specs=in_specs, out_specs=out_specs, check_vma=False)
```

profile of v0, /device:TPU:8, one launch (start us, length us, event | category | flops | bytes accessed | tf_op | source)
XLA Modules:
  0.0 299.7 jit_solution(14227140690207375910)
XLA Ops:
  6.5 1.0 fusion.9
  7.5 10.5 %psum.21 = f32[1024]{0:T(1024)S(1)} all-reduce(f32[1024]{0:T(1024)S(1)} %fusion.9), channel_id=1, replica_groups=mesh['row'=64,'col'=4] {'col'}, use_global_device_ids=true, to_apply=%region_1.2 | all-reduce | flops 1024 | bytes 8192 | tf_op jit(solution)/shard_map/psum | solution.py:30
  18.0 0.9 fusion.10
  19.2 0.9 reshape.66
  20.2 0.8 copy.14
  21.7 1.0 slice_bitcast_fusion.1
  22.7 0.8 copy.24
  25.6 77.1 %all-gather.3.cloned.1.call-done = bf16[512,8192]{1,0:T(8,128)(2,1)} async-done(((bf16[8,8192]{1,0:T(8,128)(2,1)}), bf16[512,8192]{1,0:T(8,128)(2,1)}) %all-gather.3.cloned.1.call-update) | async-done | bytes 8388624 | tf_op jit(solution)/shard_map/all_gather | solution.py:49
  102.7 9.0 %gather_fusion = bf16[160,8192]{1,0:T(8,128)(2,1)S(1)} fusion(bf16[512,8192]{1,0:T(8,128)(2,1)} %all-gather.3.cloned.1.call-done, s32[1024]{0:T(1024)S(1)} %pad_clamp_fusion), kind=kCustom, calls=%fused_computation.clone | custom fusion | bytes 5243520 | tf_op jit(solution)/shard_map/jit(_take)/gather | solution.py:53
  111.8 1.8 broadcast_select_fusion.1
  113.6 8.4 %reshape.67 = bf16[160,128,64]{2,1,0:T(8,128)(2,1)} reshape(bf16[160,8192]{1,0:T(8,128)(2,1)} %broadcast_select_fusion.1) | data formatting | bytes 5242880 | tf_op jit(solution)/shard_map/reshape | solution.py:53
  122.0 7.7 %convolution_bitcast_fusion.1 = f32[160,128,64]{1,2,0:T(8,128)S(1)} fusion(bf16[160,128,64]{2,1,0:T(8,128)(2,1)} %reshape.67, bf16[160,128,128]{2,1,0:T(8,128)(2,1)} %param.11), kind=kOutput, calls=%fused_computation.9 | convolution fusion | flops 335544320 | bytes 13107200 | tf_op jit(solution)/shard_map/tij,tjf->tif/dot_general | solution.py:50
  129.8 4.7 %fusion.14 = (f32[8,128]{1,0:T(8,128)S(1)}, f32[8,128,64]{1,0,2:T(8,128)S(1)}) fusion(f32[8,8,8,128]{3,2,1,0:T(8,128)S(1)} %copy-done.3, f32[160,128,64]{1,2,0:T(8,128)S(1)} %convolution_bitcast_fusion.1, s32[160]{0:T(256)S(1)} %bitcast.59, pred[160]{0:T(512)(128)(4,1)S(1)} %copy-done.8), kind=kOutput, calls=%fused_computation.25 | convolution fusion | flops 126027264 | bytes 5772064 | tf_op jit(solution)/shard_map/tr,tif->rif/dot_general | solution.py:56
  134.8 10.4 %psum.22 = f32[1024]{0:T(1024)S(1)} all-reduce(f32[1024]{0:T(1024)S(1)} %bitcast.55), channel_id=1, replica_groups=mesh['row'=64,'col'=4] {'col'}, use_global_device_ids=true, to_apply=%region_4.6 | all-reduce | flops 1024 | bytes 8192 | tf_op jit(solution)/shard_map/psum | solution.py:30
  149.4 76.1 %all-gather.5.cloned.1.call-done = bf16[512,8192]{1,0:T(8,128)(2,1)} async-done(((bf16[8,8192]{1,0:T(8,128)(2,1)}), bf16[512,8192]{1,0:T(8,128)(2,1)}) %all-gather.5.cloned.1.call-update) | async-done | bytes 8388624 | tf_op jit(solution)/shard_map/all_gather | solution.py:49
  225.4 9.0 %gather_fusion.1 = bf16[160,8192]{1,0:T(8,128)(2,1)S(1)} fusion(bf16[512,8192]{1,0:T(8,128)(2,1)} %all-gather.5.cloned.1.call-done, s32[1024]{0:T(1024)S(1)} %pad_clamp_fusion), kind=kCustom, calls=%fused_computation.1.clone | custom fusion | bytes 5243520 | tf_op jit(solution)/shard_map/jit(_take)/gather | solution.py:53
  234.5 1.8 broadcast_select_fusion
  236.3 8.4 %reshape.70 = bf16[160,128,64]{2,1,0:T(8,128)(2,1)} reshape(bf16[160,8192]{1,0:T(8,128)(2,1)} %broadcast_select_fusion) | data formatting | bytes 5242880 | tf_op jit(solution)/shard_map/reshape | solution.py:53
  244.7 7.7 %convolution_bitcast_fusion = f32[160,128,64]{1,2,0:T(8,128)S(1)} fusion(bf16[160,128,64]{2,1,0:T(8,128)(2,1)} %reshape.70, bf16[160,128,128]{2,1,0:T(8,128)(2,1)} %param.11), kind=kOutput, calls=%fused_computation.8 | convolution fusion | flops 335544320 | bytes 13107200 | tf_op jit(solution)/shard_map/tij,tjf->tif/dot_general | solution.py:50
  252.5 4.7 %fusion.12 = (f32[8,128]{1,0:T(8,128)S(1)}, f32[8,128,64]{1,0,2:T(8,128)S(1)}) fusion(f32[8,8,8,128]{3,2,1,0:T(8,128)S(1)} %copy-done.4, f32[160,128,64]{1,2,0:T(8,128)S(1)} %convolution_bitcast_fusion, s32[160]{0:T(256)S(1)} %bitcast.60, pred[160]{0:T(512)(128)(4,1)S(1)} %copy-done.9), kind=kOutput, calls=%fused_computation.22 | convolution fusion | flops 126027264 | bytes 5772064 | tf_op jit(solution)/shard_map/tr,tif->rif/dot_general | solution.py:56
  257.3 10.4 %psum.23 = f32[1024]{0:T(1024)S(1)} all-reduce(f32[1024]{0:T(1024)S(1)} %bitcast.56), channel_id=1, replica_groups=mesh['row'=64,'col'=4] {'col'}, use_global_device_ids=true, to_apply=%region_6.8 | all-reduce | flops 1024 | bytes 8192 | tf_op jit(solution)/shard_map/psum | solution.py:30
  267.8 1.3 convolution_bitcast_fusion.2
  269.1 22.4 %reduce-scatter.2.cloned.1.call-done = f32[1024,64]{0,1:T(8,128)} async-done(((f32[1024,256]{0,1:T(8,128)}), f32[1024,64]{0,1:T(8,128)}) %reduce-scatter.2.cloned.1.call-update) | async-done | bytes 262160 | tf_op jit(solution)/shard_map/reduce_scatter | solution.py:64
  291.5 1.6 convert_element_type.26
  (50 shorter events, 7.0 us)
Async XLA Ops:
  6.5 261.2 %copy-start = (bf16[3,256,256]{2,1,0:T(8,128)(2,1)S(1)}, bf16[3,256,256]{2,1,0:T(8,128)(2,1)}, u32[]{:S(2)}) copy-start(bf16[3,256,256]{2,1,0:T(8,128)(2,1)} %param.17) | copy-start | bytes 1179652
  6.5 96.2 %all-gather.3.cloned.1.call-start = ((), (), s32[]{:S(2)}) async-start(), calls=%async_computation.1 | async-start | bytes 8519680 | tf_op jit(solution)/shard_map/all_gather | solution.py:49
  20.1 205.3 %all-gather.5.cloned.1.call-start = ((), (), s32[]{:S(2)}) async-start(), calls=%async_computation.2 | async-start | bytes 8519680 | tf_op jit(solution)/shard_map/all_gather | solution.py:49
  122.0 7.7 %copy-start.3 = (f32[8,8,8,128]{3,2,1,0:T(8,128)S(1)}, f32[8,8,8,128]{3,2,1,0:T(8,128)}, u32[]{:S(2)}) copy-start(f32[8,8,8,128]{3,2,1,0:T(8,128)} %copy.24) | copy-start | bytes 786436
  122.0 7.7 %copy-start.7 = (s32[1,160]{1,0:T(1,128)S(1)}, s32[1,160]{1,0:T(1,128)}, u32[]{:S(2)}) copy-start(s32[1,160]{1,0:T(1,128)} %param.12) | copy-start | bytes 1924
  122.0 7.7 %copy-start.8 = (pred[160]{0:T(512)(128)(4,1)S(1)}, pred[160]{0:T(512)(128)(4,1)}, u32[]{:S(2)}) copy-start(pred[160]{0:T(512)(128)(4,1)} %iota_compare_fusion.2) | copy-start | bytes 484
  129.7 15.5 %copy-start.1 = (f32[2,1024,64]{1,2,0:T(8,128)S(1)}, f32[2,1024,64]{1,2,0:T(8,128)}, u32[]{:S(2)}) copy-start(f32[2,1024,64]{1,2,0:T(8,128)} %param.16) | copy-start | bytes 1572868
  129.8 18.2 %copy-start.2 = (bf16[1024,64]{0,1:T(8,128)(2,1)S(1)}, bf16[1024,64]{0,1:T(8,128)(2,1)}, u32[]{:S(2)}) copy-start(bf16[1024,64]{0,1:T(8,128)(2,1)} %param.10) | copy-start | bytes 393220
  147.6 143.9 %reduce-scatter.2.cloned.1.call-start = ((), (), s32[]{:S(2)}) async-start(), calls=%async_computation.3 | async-start | bytes 1310720 | tf_op jit(solution)/shard_map/reduce_scatter | solution.py:64
  244.7 7.7 %copy-start.4 = (f32[8,8,8,128]{3,2,1,0:T(8,128)S(1)}, f32[8,8,8,128]{3,2,1,0:T(8,128)}, u32[]{:S(2)}) copy-start(f32[8,8,8,128]{3,2,1,0:T(8,128)} %copy.25) | copy-start | bytes 786436
  244.7 7.7 %copy-start.9 = (pred[160]{0:T(512)(128)(4,1)S(1)}, pred[160]{0:T(512)(128)(4,1)}, u32[]{:S(2)}) copy-start(pred[160]{0:T(512)(128)(4,1)} %iota_compare_fusion.2) | copy-start | bytes 484
  252.4 15.3 %copy-start.5 = (bf16[1,1024,64]{1,2,0:T(8,128)(2,1)S(1)}, bf16[1,1024,64]{1,2,0:T(8,128)(2,1)}, u32[]{:S(2)}) copy-start(bf16[1,1024,64]{1,2,0:T(8,128)(2,1)} %fusion.31) | copy-start | bytes 393220
  252.4 15.3 %copy-start.6 = (bf16[1,1024,64]{1,2,0:T(8,128)(2,1)S(1)}, bf16[1,1024,64]{1,2,0:T(8,128)(2,1)}, u32[]{:S(2)}) copy-start(bf16[1,1024,64]{1,2,0:T(8,128)(2,1)} %get-tuple-element.8) | copy-start | bytes 393220
Sparse Core Ops, SparseCore 0:
  20.2 82.4 all-gather.2
  147.8 77.6 all-gather.4
  269.3 22.2 reduce-scatter.1
where the time goes:
time: 300 us
  waiting for transfers between devices  176 us (59%)
  local copies, waits for them, and re-layouts  40.7 us (14%)
  blocking collectives  31.4 us (10%)
  matrix products  26.2 us (9%)
  between operations  14 us (5%)
  other arithmetic  11.5 us (4%)
    all_gather x2, waiting for transfers between devices, shards(): lax.all_gather(current.reshape(BPD, BLK * local_width), 'row', axis=0, ti...  153 us
    psum x3, blocking collectives, normalize(): squares = lax.psum(jnp.sum(values * values, axis=1), 'col')  31.4 us
    reduce_scatter x1, waiting for transfers between devices, shards(): encoded = lax.psum_scatter(terms, 'col', scatter_dimension=1, tiled=True)  22.4 us
    gather x2, local copies, waits for them, and re-layouts, shards(): jnp.take(whole, global_block, axis=0).reshape(TPD, BLK, local_width)  18.1 us
    reshape x2, local copies, waits for them, and re-layouts, shards(): jnp.take(whole, global_block, axis=0).reshape(TPD, BLK, local_width)  16.8 us
    dot_general x2, matrix products, shards(): jnp.einsum('tij,tjf->tif', tile_vals, jnp.take(whole, global_block, axis=...  15.4 us
    dot_general x2, matrix products, shards(): jnp.einsum('tr,tif->rif', onehot, products, precision=lax.Precision.HIGHEST)  9.47 us
  transfers between devices with their start and end apart: 3, of which 3 were waited for; matrix products, arithmetic and copies ran while one was open for 2% of the time, Pallas kernels for 0%

commit v1 on v0

--- a/solution.py
+++ b/solution.py
@@ -46,7 +46,15 @@
     current = normalize(features.astype(jnp.float32))
     layers = [current]
     for hop_index in range(HOPS):
-        whole = lax.all_gather(current.reshape(BPD, BLK * local_width), "row", axis=0, tiled=True)
+        whole = jnp.concatenate(
+            lax.all_to_all(
+                jnp.stack([current.reshape(BPD, BLK * local_width)] * lax.axis_size("row")),
+                "row",
+                0,
+                0,
+            ),
+            axis=0,
+        )
         products = jnp.einsum(
             "tij,tjf->tif",
             tile_vals,

time: 300 us -> 532 us (1.77)
  waiting for transfers between devices: 176 us -> 387 us
  starting transfers between devices: 0.31 us -> 20.2 us
  local copies, waits for them, and re-layouts: 40.7 us -> 46.8 us
    all_to_all x0 -> x2, waiting for transfers between devices: none -> 364 us  [shards(): lax.all_to_all(jnp.stack([current.reshape(BPD, BLK * local_width)] * lax....]
    all_gather x2 -> x0, waiting for transfers between devices: 153 us -> none  [shards(): lax.all_gather(current.reshape(BPD, BLK * local_width), 'row', axis=0, ti...]
    all_to_all x0 -> x2, starting transfers between devices: none -> 19.9 us  [shards(): lax.all_to_all(jnp.stack([current.reshape(BPD, BLK * local_width)] * lax....]
    another operation x0 -> x3, local copies, waits for them, and re-layouts: none -> 8.73 us  [shards(): jnp.stack([current.reshape(BPD, BLK * local_width)] * lax.axis_size('row'))]
  transfers between devices with their start and end apart: 3 -> 3, of which waited for: 3 -> 3; matrix products, arithmetic and copies ran while one was open for 2% -> 1% of each run, Pallas kernels for 0% -> 0%
where the time goes in v1:
time: 532 us
  waiting for transfers between devices  387 us (73%)
  local copies, waits for them, and re-layouts  46.8 us (9%)
  blocking collectives  28 us (5%)
  matrix products  26.2 us (5%)
  starting transfers between devices  20.2 us (4%)
  between operations  14.3 us (3%)
  other arithmetic  9.51 us (2%)
    all_to_all x2, waiting for transfers between devices, shards(): lax.all_to_all(jnp.stack([current.reshape(BPD, BLK * local_width)] * lax....  364 us
    psum x3, blocking collectives, normalize(): squares = lax.psum(jnp.sum(values * values, axis=1), 'col')  28 us
    reduce_scatter x1, waiting for transfers between devices, shards(): encoded = lax.psum_scatter(terms, 'col', scatter_dimension=1, tiled=True)  22.2 us
    all_to_all x2, starting transfers between devices, shards(): lax.all_to_all(jnp.stack([current.reshape(BPD, BLK * local_width)] * lax....  19.9 us
    gather x2, local copies, waits for them, and re-layouts, shards(): jnp.take(whole, global_block, axis=0).reshape(TPD, BLK, local_width)  18.1 us
    reshape x2, local copies, waits for them, and re-layouts, shards(): jnp.take(whole, global_block, axis=0).reshape(TPD, BLK, local_width)  16.8 us
    dot_general x2, matrix products, shards(): jnp.einsum('tij,tjf->tif', tile_vals, jnp.take(whole, global_block, axis=...  15.4 us
  transfers between devices with their start and end apart: 3, of which 3 were waited for; matrix products, arithmetic and copies ran while one was open for 1% of the time, Pallas kernels for 0%

profile of v1, /device:TPU:8, one launch (start us, length us, event | category | flops | bytes accessed | tf_op | source)
XLA Modules:
  0.0 531.6 jit_solution(4693057574266179005)
XLA Ops:
  6.5 1.0 fusion.9
  7.5 10.5 %psum.21 = f32[1024]{0:T(1024)S(1)} all-reduce(f32[1024]{0:T(1024)S(1)} %fusion.9), channel_id=1, replica_groups=mesh['row'=64,'col'=4] {'col'}, use_global_device_ids=true, to_apply=%region_1.2 | all-reduce | flops 1024 | bytes 8192 | tf_op jit(solution)/shard_map/psum | solution.py:30
  18.0 0.9 fusion.10
  19.4 4.2 stack.15
  23.7 12.4 %all-to-all-start = ((bf16[64,8,8192]{2,1,0:T(8,128)(2,1)}), bf16[64,8,8192]{2,1,0:T(8,128)(2,1)}, u32[]{:S(2)}, u32[]{:S(2)}) async-start(bf16[64,8,8192]{2,1,0:T(8,128)(2,1)} %stack.15), calls=%async_computation | async-start | bytes 16777216 | tf_op jit(solution)/shard_map/all_to_all | solution.py:50
  38.6 181.8 %all-to-all-done = bf16[64,8,8192]{2,1,0:T(8,128)(2,1)} async-done(((bf16[64,8,8192]{2,1,0:T(8,128)(2,1)}), bf16[64,8,8192]{2,1,0:T(8,128)(2,1)}, u32[]{:S(2)}, u32[]{:S(2)}) %all-to-all-start) | async-done | bytes 8388640 | tf_op jit(solution)/shard_map/all_to_all | solution.py:50
  220.3 9.0 %gather_fusion = bf16[160,8192]{1,0:T(8,128)(2,1)S(1)} fusion(bf16[512,8192]{1,0:T(8,128)(2,1)} %bitcast.6, s32[1024]{0:T(1024)S(1)} %pad_clamp_fusion), kind=kCustom, calls=%fused_computation.clone | custom fusion | bytes 5243520 | tf_op jit(solution)/shard_map/jit(_take)/gather | solution.py:61
  229.4 1.8 broadcast_select_fusion.1
  231.2 8.4 %reshape.78 = bf16[160,128,64]{2,1,0:T(8,128)(2,1)} reshape(bf16[160,8192]{1,0:T(8,128)(2,1)} %broadcast_select_fusion.1) | data formatting | bytes 5242880 | tf_op jit(solution)/shard_map/reshape | solution.py:61
  239.6 7.7 %convolution_bitcast_fusion.1 = f32[160,128,64]{1,2,0:T(8,128)S(1)} fusion(bf16[160,128,64]{2,1,0:T(8,128)(2,1)} %reshape.78, bf16[160,128,128]{2,1,0:T(8,128)(2,1)} %param.11), kind=kOutput, calls=%fused_computation.9 | convolution fusion | flops 335544320 | bytes 13107200 | tf_op jit(solution)/shard_map/tij,tjf->tif/dot_general | solution.py:58
  247.4 4.7 fusion.14
  252.4 7.8 %psum.22 = f32[1024]{0:T(1024)S(1)} all-reduce(f32[1024]{0:T(1024)S(1)} %bitcast.57), channel_id=1, replica_groups=mesh['row'=64,'col'=4] {'col'}, use_global_device_ids=true, to_apply=%region_4.6 | all-reduce | flops 1024 | bytes 8192 | tf_op jit(solution)/shard_map/psum | solution.py:30
  261.9 4.2 stack.16
  266.1 7.5 %all-to-all-start.1 = ((bf16[64,8,8192]{2,1,0:T(8,128)(2,1)}), bf16[64,8,8192]{2,1,0:T(8,128)(2,1)}, u32[]{:S(2)}, u32[]{:S(2)}) async-start(bf16[64,8,8192]{2,1,0:T(8,128)(2,1)} %stack.16), calls=%async_computation.1 | async-start | bytes 16777216 | tf_op jit(solution)/shard_map/all_to_all | solution.py:50
  275.3 182.5 %all-to-all-done.1 = bf16[64,8,8192]{2,1,0:T(8,128)(2,1)} async-done(((bf16[64,8,8192]{2,1,0:T(8,128)(2,1)}), bf16[64,8,8192]{2,1,0:T(8,128)(2,1)}, u32[]{:S(2)}, u32[]{:S(2)}) %all-to-all-start.1) | async-done | bytes 8388640 | tf_op jit(solution)/shard_map/all_to_all | solution.py:50
  457.9 9.0 %gather_fusion.1 = bf16[160,8192]{1,0:T(8,128)(2,1)S(1)} fusion(bf16[512,8192]{1,0:T(8,128)(2,1)} %bitcast.10, s32[1024]{0:T(1024)S(1)} %pad_clamp_fusion), kind=kCustom, calls=%fused_computation.1.clone | custom fusion | bytes 5243520 | tf_op jit(solution)/shard_map/jit(_take)/gather | solution.py:61
  466.9 1.8 broadcast_select_fusion
  468.7 8.4 %reshape.82 = bf16[160,128,64]{2,1,0:T(8,128)(2,1)} reshape(bf16[160,8192]{1,0:T(8,128)(2,1)} %broadcast_select_fusion) | data formatting | bytes 5242880 | tf_op jit(solution)/shard_map/reshape | solution.py:61
  477.1 7.7 %convolution_bitcast_fusion = f32[160,128,64]{1,2,0:T(8,128)S(1)} fusion(bf16[160,128,64]{2,1,0:T(8,128)(2,1)} %reshape.82, bf16[160,128,128]{2,1,0:T(8,128)(2,1)} %param.11), kind=kOutput, calls=%fused_computation.8 | convolution fusion | flops 335544320 | bytes 13107200 | tf_op jit(solution)/shard_map/tij,tjf->tif/dot_general | solution.py:58
  484.9 4.7 fusion.12
  489.7 9.8 %psum.23 = f32[1024]{0:T(1024)S(1)} all-reduce(f32[1024]{0:T(1024)S(1)} %bitcast.58), channel_id=1, replica_groups=mesh['row'=64,'col'=4] {'col'}, use_global_device_ids=true, to_apply=%region_6.8 | all-reduce | flops 1024 | bytes 8192 | tf_op jit(solution)/shard_map/psum | solution.py:30
  499.5 1.3 convolution_bitcast_fusion.2
  500.9 22.2 %reduce-scatter.2.cloned.1.call-done = f32[1024,64]{0,1:T(8,128)} async-done(((f32[1024,256]{0,1:T(8,128)}), f32[1024,64]{0,1:T(8,128)}) %reduce-scatter.2.cloned.1.call-update) | async-done | bytes 262160 | tf_op jit(solution)/shard_map/reduce_scatter | solution.py:72
  523.1 1.6 convert_element_type.27
  (54 shorter events, 6.1 us)
Async XLA Ops:
  6.5 493.0 %copy-start = (bf16[3,256,256]{2,1,0:T(8,128)(2,1)S(1)}, bf16[3,256,256]{2,1,0:T(8,128)(2,1)}, u32[]{:S(2)}) copy-start(bf16[3,256,256]{2,1,0:T(8,128)(2,1)} %param.17) | copy-start | bytes 1179652
  23.7 12.5 %copy-start.10 = (s32[1,64,2]{1,2,0:T(2,128)S(1)}, s32[1,64,2]{1,2,0:T(2,128)}, u32[]{:S(2)}) copy-start(s32[1,64,2]{1,2,0:T(2,128)} %param.15) | copy-start | bytes 1540
  23.7 13.4 %copy-start.1 = (f32[2,1024,64]{1,2,0:T(8,128)S(1)}, f32[2,1024,64]{1,2,0:T(8,128)}, u32[]{:S(2)}) copy-start(f32[2,1024,64]{1,2,0:T(8,128)} %param.16) | copy-start | bytes 1572868
  23.7 14.7 %copy-start.11 = (s32[1,160]{1,0:T(1,128)S(1)}, s32[1,160]{1,0:T(1,128)}, u32[]{:S(2)}) copy-start(s32[1,160]{1,0:T(1,128)} %param.13) | copy-start | bytes 1924
  23.7 196.7 %all-to-all-start = ((bf16[64,8,8192]{2,1,0:T(8,128)(2,1)}), bf16[64,8,8192]{2,1,0:T(8,128)(2,1)}, u32[]{:S(2)}, u32[]{:S(2)}) async-start(bf16[64,8,8192]{2,1,0:T(8,128)(2,1)} %stack.15), calls=%async_computation | async-start | bytes 16777216 | tf_op jit(solution)/shard_map/all_to_all | solution.py:50
  239.6 7.7 %copy-start.3 = (f32[8,8,8,128]{3,2,1,0:T(8,128)S(1)}, f32[8,8,8,128]{3,2,1,0:T(8,128)}, u32[]{:S(2)}) copy-start(f32[8,8,8,128]{3,2,1,0:T(8,128)} %copy.24) | copy-start | bytes 786436
  239.6 7.7 %copy-start.7 = (s32[1,160]{1,0:T(1,128)S(1)}, s32[1,160]{1,0:T(1,128)}, u32[]{:S(2)}) copy-start(s32[1,160]{1,0:T(1,128)} %param.12) | copy-start | bytes 1924
  239.6 7.7 %copy-start.8 = (pred[160]{0:T(512)(128)(4,1)S(1)}, pred[160]{0:T(512)(128)(4,1)}, u32[]{:S(2)}) copy-start(pred[160]{0:T(512)(128)(4,1)} %iota_compare_fusion.2) | copy-start | bytes 484
  266.1 7.8 %copy-start.2 = (bf16[1024,64]{0,1:T(8,128)(2,1)S(1)}, bf16[1024,64]{0,1:T(8,128)(2,1)}, u32[]{:S(2)}) copy-start(bf16[1024,64]{0,1:T(8,128)(2,1)} %param.10) | copy-start | bytes 393220
  266.1 191.8 %all-to-all-start.1 = ((bf16[64,8,8192]{2,1,0:T(8,128)(2,1)}), bf16[64,8,8192]{2,1,0:T(8,128)(2,1)}, u32[]{:S(2)}, u32[]{:S(2)}) async-start(bf16[64,8,8192]{2,1,0:T(8,128)(2,1)} %stack.16), calls=%async_computation.1 | async-start | bytes 16777216 | tf_op jit(solution)/shard_map/all_to_all | solution.py:50
  273.6 249.5 %reduce-scatter.2.cloned.1.call-start = ((), (), s32[]{:S(2)}) async-start(), calls=%async_computation.3 | async-start | bytes 1310720 | tf_op jit(solution)/shard_map/reduce_scatter | solution.py:72
  477.1 7.7 %copy-start.4 = (f32[8,8,8,128]{3,2,1,0:T(8,128)S(1)}, f32[8,8,8,128]{3,2,1,0:T(8,128)}, u32[]{:S(2)}) copy-start(f32[8,8,8,128]{3,2,1,0:T(8,128)} %copy.25) | copy-start | bytes 786436
  477.1 7.7 %copy-start.9 = (pred[160]{0:T(512)(128)(4,1)S(1)}, pred[160]{0:T(512)(128)(4,1)}, u32[]{:S(2)}) copy-start(pred[160]{0:T(512)(128)(4,1)} %iota_compare_fusion.2) | copy-start | bytes 484
  484.9 14.6 %copy-start.5 = (bf16[1,1024,64]{1,2,0:T(8,128)(2,1)S(1)}, bf16[1,1024,64]{1,2,0:T(8,128)(2,1)}, u32[]{:S(2)}) copy-start(bf16[1,1024,64]{1,2,0:T(8,128)(2,1)} %fusion.31) | copy-start | bytes 393220
  484.9 14.6 %copy-start.6 = (bf16[1,1024,64]{1,2,0:T(8,128)(2,1)S(1)}, bf16[1,1024,64]{1,2,0:T(8,128)(2,1)}, u32[]{:S(2)}) copy-start(bf16[1,1024,64]{1,2,0:T(8,128)(2,1)} %get-tuple-element.8) | copy-start | bytes 393220
Sparse Core Ops, SparseCore 0:
  501.0 22.0 reduce-scatter.1
